TPU v7x, 128 devices: a whole 4x4x4 slice. The times are simulated.
128 devices in a mesh: frames: 32 (over x, y, core), slabs: 4 (over z).
Axes of the slice: x: 4, y: 4, z: 4, core: 2. Of those that a mesh axis runs over, the one named last changes fastest.
Arguments:
- frame_pixels: float32 [256, 384, 1024], P('frames', 'slabs'), may hold values from -6 to 6
- bragg_mask: int32 [256, 384, 1024], P('frames', 'slabs'), may hold values 0 or 1
- interp: bfloat16 [4, 4096, 1024], P('slabs'), may hold values from -0.09375 to 0.09375
- block_list: int32 [256, 4, 96], P('frames', 'slabs'), may hold values from 0 to 4095, as said below
- owner_map: int32 [4, 4096], P('slabs'), may hold values from 0 to 4095, as said below
- mirror_pair: int32 [4, 128], P('slabs'), may hold values from 0 to 127, as said below
Outputs:
- merged: float32 [4, 4096, 1024], P('slabs', 'frames')
Inputs may be any that keep to these rules, and one draw needn't show every extreme that they name: `block_list`: among the list entries of the frames of one frame group in one slab group, at most 48 name blocks whose position lies in one owner's range of 128 positions, and in every such set some owner receives exactly 48. `owner_map`: each row is a permutation of the block numbers. `mirror_pair`: each row is a permutation; the row of slab group s xor (2) is the inverse of the row of s, so pairs are mutual.
All inputs are finite; a program needn't handle non-finite values. No bound on the sum of `bragg_mask` on one device may be relied on, other than what follows from the above.
Results may differ from a plain program's by a relative error of at most 0.0029.
Values may be sent and summed in bfloat16 or wider, within the bound.
A program may use at most 128 MiB of HBM per device.

v0:
```python
import jax
import jax.numpy as jnp
from jax import lax
from jax.sharding import PartitionSpec as P

PANEL_ROWS = 4
RADIUS = 4


EPSILON = 1e-05


def extended(cells, sides, width):
    for axis, dim in sides:
        count = lax.axis_size(axis)
        ends = count - 1
        head = lax.slice_in_dim(cells, 0, width, axis=dim)
        tail = lax.slice_in_dim(cells, cells.shape[dim] - width, cells.shape[dim], axis=dim)
        cells = jnp.concatenate(
            [
                lax.ppermute(tail, axis, [(i, (i + 1) % count) for i in range(ends)]),
                cells,
                lax.ppermute(head, axis, [((i + 1) % count, i) for i in range(ends)]),
            ],
            axis=dim,
        )
    return cells


def partner_2(block, axis, apart):
    count = lax.axis_size(axis)
    route = []
    for low in range(count):
        high = low | 1 << apart
        if high != low and high < count:
            route += [(low, high), (high, low)]
    return lax.ppermute(block, axis, route)


def box_total(padded, row_count, col_count):
    box_width = 2 * RADIUS + 1
    row_sums = padded[:, 0:row_count, :]
    for offset in range(1, box_width):
        row_sums = row_sums + padded[:, offset : offset + row_count, :]
    full_sums = row_sums[:, :, 0:col_count]
    for offset in range(1, box_width):
        full_sums = full_sums + row_sums[:, :, offset : offset + col_count]
    return full_sums


def normalize(pixels, mask, row_padded):
    row_count = pixels.shape[1]
    col_count = pixels.shape[2]
    padded = jnp.pad(row_padded, ((0, 0), (0, 0), (RADIUS, RADIUS)))
    plain_sums = box_total(padded, row_count, col_count)
    square_sums = box_total(padded * padded, row_count, col_count)
    box_area = (2 * RADIUS + 1) * (2 * RADIUS + 1)
    box_mean = plain_sums / box_area
    box_var = square_sums / box_area - box_mean * box_mean
    scaled = (pixels - box_mean) * lax.rsqrt(box_var + EPSILON)
    return jnp.where(mask == 1, jnp.zeros_like(scaled), scaled).astype(jnp.bfloat16)


def shards(frame_pixels, bragg_mask, interp, block_list, owner_map, mirror_pair):
    row_padded = extended(frame_pixels, (("slabs", 1),), RADIUS)
    corrected = normalize(frame_pixels, bragg_mask, row_padded)
    frame_count, local_rows, col_count = corrected.shape
    panel_values = corrected.reshape(frame_count, local_rows // PANEL_ROWS, PANEL_ROWS * col_count)
    weights = interp[0]
    panel_piece = lax.all_gather(panel_values, "slabs", axis=1, tiled=True)
    piece_frames, piece_panels, piece_width = panel_piece.shape
    flat_rows = panel_piece.reshape(piece_frames * piece_panels, piece_width)
    product = jnp.dot(flat_rows, weights, preferred_element_type=jnp.float32)
    contrib = product.reshape(piece_frames, piece_panels, product.shape[1])
    voxel_count = contrib.shape[2]
    entry_count = contrib.shape[0] * contrib.shape[1]
    flat_terms = contrib.reshape(entry_count, voxel_count)
    listed = block_list[:, 0, :].reshape(entry_count)
    position = owner_map[0][listed]
    dense_terms = jax.ops.segment_sum(flat_terms, position, num_segments=owner_map.shape[1])
    owned = lax.psum_scatter(dense_terms, "frames", scatter_dimension=0, tiled=True)
    bit_number = lax.axis_size("slabs").bit_length() - 2
    partner = partner_2(owned, "slabs", bit_number)
    paired = partner[mirror_pair[0]][:, ::-1]
    merged = 0.5 * (owned + paired)
    return merged[None]


def solution(mesh):
    return jax.shard_map(
        shards,
        mesh=mesh,
        in_specs=(
            P("frames", "slabs", None),
            P("frames", "slabs", None),
            P("slabs", None, None),
            P("frames", "slabs", None),
            P("slabs", None),
            P("slabs", None),
        ),
        out_specs=P("slabs", "frames", None),
        check_vma=False,
    )
```

profile of v0, /device:TPU:1, one launch (start us, length us, event | category | flops | bytes accessed | tf_op | source)
XLA Modules:
  0.0 307.1 jit_solution(16130094358181146046)
XLA Ops:
  6.5 0.0 copy-start
  6.5 0.0 all-gather.2.cloned.1.call-start
  6.5 1.1 fusion.16
  7.6 4.4 %collective-permute-start = (f32[8,4,1024]{2,1,0:T(4,128)S(1)}, f32[8,4,1024]{2,1,0:T(4,128)S(1)}, u32[]{:S(2)}, u32[]{:S(2)}) collective-permute-start(f32[8,4,1024]{2,1,0:T(4,128)S(1)} %get-tuple-element.7), channel_id=1, source_target_pairs={{0,1},{1,2},{2,3},{4,5},{5,6},{6,7},{8,9},{9,10},{10,11},{12,13},{... | collective-permute-start | bytes 393224 | tf_op jit(solution)/shard_map/ppermute | solution.py:21
  12.0 1.3 collective-permute-start.1
  13.3 0.8 collective-permute-done
  14.2 4.2 %collective-permute-done.1 = f32[8,4,1024]{2,1,0:T(4,128)S(1)} collective-permute-done((f32[8,4,1024]{2,1,0:T(4,128)S(1)}, f32[8,4,1024]{2,1,0:T(4,128)S(1)}, u32[]{:S(2)}, u32[]{:S(2)}) %collective-permute-start.1) | collective-permute-done | bytes 131104 | tf_op jit(solution)/shard_map/ppermute | solution.py:23
  18.3 5.2 %select_maximum_fusion = (f32[8,104,1032]{2,1,0:T(8,128)S(1)}, f32[8,104,1032]{2,1,0:T(8,128)}) fusion(f32[8,4,1024]{2,1,0:T(4,128)S(1)} %collective-permute-done.1, f32[8,96,1024]{2,1,0:T(8,128)} %param.6, f32[8,4,1024]{2,1,0:T(4,128)S(1)} %collective-permute-done), kind=kLoop, calls=%fused_computation.9 | loop fusion | flops 7727616 | bytes 10276864 | tf_op jit(solution)/shard_map/concatenate | solution.py:19
  23.6 17.4 %slice_add_fusion = (f32[8,96,1032]{2,1,0:T(8,128)}, f32[8,96,1032]{2,1,0:T(8,128)}) fusion(f32[8,104,1032]{2,1,0:T(8,128)} %get-tuple-element.6, f32[8,104,1032]{2,1,0:T(8,128)S(1)} %get-tuple-element.5), kind=kLoop, calls=%fused_computation.12 | loop fusion | flops 12681216 | bytes 63406080 | tf_op jit(solution)/shard_map/add | solution.py:44
  40.9 31.0 %fusion.11 = bf16[8,96,1024]{2,1,0:T(8,128)(2,1)S(1)} fusion(f32[8,96,1032]{2,1,0:T(8,128)} %get-tuple-element.9, f32[8,96,1024]{2,1,0:T(8,128)} %param.6, f32[8,96,1032]{2,1,0:T(8,128)} %get-tuple-element.10, s32[8,96,1024]{2,1,0:T(8,128)} %param.7), kind=kLoop, calls=%fused_computation.35 | loop fusion | flops 20447232 | bytes 64487424 | tf_op jit(solution)/shard_map/convert_element_type | solution.py:61
  71.9 0.0 copy-start.2
  71.9 2.2 reshape.62
  74.1 0.0 all-gather.2.cloned.1.call-update
  74.2 0.2 reduce-scatter.2.cloned.1.call-start
  74.4 0.5 broadcast.67
  74.9 0.0 copy-done.2
  74.9 0.7 reduce.5
  75.6 0.1 reshape_squeeze.3
  75.7 0.0 copy-done
  75.7 4.5 %gather_fusion = s32[768]{0:T(1024)S(1)} fusion(s32[4096]{0:T(1024)S(1)} %bitcast.12, s32[1024]{0:T(1024)S(1)} %pad_clamp_fusion.1), kind=kCustom, calls=%fused_computation | custom fusion | bytes 9216 | tf_op jit(solution)/shard_map/gather | solution.py:79
  80.2 62.8 %all-gather.2.cloned.1.call-done = bf16[8,96,4096]{2,1,0:T(8,128)(2,1)} async-done(((bf16[8,24,4096]{2,1,0:T(8,128)(2,1)}), bf16[8,96,4096]{2,1,0:T(8,128)(2,1)}) %all-gather.2.cloned.1.call-update) | async-done | bytes 6291472 | tf_op jit(solution)/shard_map/all_gather | solution.py:70
  142.9 10.9 %fusion = f32[768,1024]{1,0:T(8,128)S(1)} fusion(bf16[768,4096]{1,0:T(8,128)(2,1)} %bitcast.13, bf16[1,4096,1024]{2,1,0:T(8,128)(2,1)} %param.8), kind=kOutput, calls=%fused_computation.3 | convolution fusion | flops 6442450944 | bytes 17825792 | tf_op jit(solution)/shard_map/dot_general | solution.py:73
  153.9 16.0 %scatter_custom_fusion = f32[4096,1024]{1,0:T(8,128)} fusion(s32[768]{0:T(1024)S(1)} %gather_fusion, f32[768,1024]{1,0:T(8,128)S(1)} %fusion, f32[]{:T(128)} %constant.8.clone.1), kind=kCustom, calls=%fused_computation.5 | custom fusion | flops 786432 | bytes 16777220 | tf_op jit(solution)/shard_map/scatter-add | solution.py:80
  169.9 0.0 copy-start.3
  169.9 0.0 reduce-scatter.2.cloned.1.call-update
  169.9 114.6 %reduce-scatter.2.cloned.1.call-done = f32[128,1024]{1,0:T(8,128)} async-done(((f32[4096,1024]{1,0:T(8,128)}), f32[128,1024]{1,0:T(8,128)}) %reduce-scatter.2.cloned.1.call-update) | async-done | bytes 524304 | tf_op jit(solution)/shard_map/reduce_scatter | solution.py:81
  284.5 0.0 copy-start.1
  284.5 2.9 collective-permute-start.2
  287.4 0.0 copy-done.3
  287.4 10.5 %collective-permute-done.2 = f32[128,1024]{1,0:T(8,128)S(1)} collective-permute-done((f32[128,1024]{1,0:T(8,128)}, f32[128,1024]{1,0:T(8,128)S(1)}, u32[]{:S(2)}, u32[]{:S(2)}) %collective-permute-start.2) | collective-permute-done | bytes 524320 | tf_op jit(solution)/shard_map/ppermute | solution.py:37
  297.9 0.8 gather_fusion.1
  298.7 0.8 rev.3
  299.4 0.0 copy-done.1
  299.4 0.9 multiply_bitcast_fusion
  (4 shorter events, 0.0 us)
Async XLA Ops:
  6.5 69.2 %copy-start = (s32[1,4096]{1,0:T(1,128)S(1)}, s32[1,4096]{1,0:T(1,128)}, u32[]{:S(2)}) copy-start(s32[1,4096]{1,0:T(1,128)} %param.10) | copy-start | bytes 49156
  6.5 136.4 %all-gather.2.cloned.1.call-start = ((), (), s32[]{:S(2)}) async-start(), calls=%async_computation.1 | async-start | bytes 7864320 | tf_op jit(solution)/shard_map/all_gather | solution.py:70
  7.6 6.5 %collective-permute-start = (f32[8,4,1024]{2,1,0:T(4,128)S(1)}, f32[8,4,1024]{2,1,0:T(4,128)S(1)}, u32[]{:S(2)}, u32[]{:S(2)}) collective-permute-start(f32[8,4,1024]{2,1,0:T(4,128)S(1)} %get-tuple-element.7), channel_id=1, source_target_pairs={{0,1},{1,2},{2,3},{4,5},{5,6},{6,7},{8,9},{9,10},{10,11},{12,13},{... | collective-permute-start | bytes 393224 | tf_op jit(solution)/shard_map/ppermute | solution.py:21
  12.0 6.3 %collective-permute-start.1 = (f32[8,4,1024]{2,1,0:T(4,128)S(1)}, f32[8,4,1024]{2,1,0:T(4,128)S(1)}, u32[]{:S(2)}, u32[]{:S(2)}) collective-permute-start(f32[8,4,1024]{2,1,0:T(4,128)S(1)} %get-tuple-element.8), channel_id=1, source_target_pairs={{1,0},{2,1},{3,2},{5,4},{6,5},{7,6},{9,8},{10,9},{11,10},{13,12},{... | collective-permute-start | bytes 393224 | tf_op jit(solution)/shard_map/ppermute | solution.py:23
  71.9 3.0 copy-start.2
  74.2 210.4 %reduce-scatter.2.cloned.1.call-start = ((), (), s32[]{:S(2)}) async-start(), calls=%async_computation.2 | async-start | bytes 17301504 | tf_op jit(solution)/shard_map/reduce_scatter | solution.py:81
  169.9 117.5 %copy-start.3 = (s32[1,128]{1,0:T(1,128)S(1)}, s32[1,128]{1,0:T(1,128)}, u32[]{:S(2)}) copy-start(s32[1,128]{1,0:T(1,128)} %param.11) | copy-start | bytes 1540
  284.5 14.9 %copy-start.1 = (f32[128,1024]{1,0:T(8,128)S(1)}, f32[128,1024]{1,0:T(8,128)}, u32[]{:S(2)}) copy-start(f32[128,1024]{1,0:T(8,128)} %reduce-scatter.2.cloned.1.call-done) | copy-start | bytes 1572868
  284.5 13.3 %collective-permute-start.2 = (f32[128,1024]{1,0:T(8,128)}, f32[128,1024]{1,0:T(8,128)S(1)}, u32[]{:S(2)}, u32[]{:S(2)}) collective-permute-start(f32[128,1024]{1,0:T(8,128)} %reduce-scatter.2.cloned.1.call-done), channel_id=1, source_target_pairs={{0,2},{2,0},{1,3},{3,1},{4,6},{6,4},{5,7},{7,5},{8,10},{10,8},{9,1... | collective-permute-start | bytes 1572872 | tf_op jit(solution)/shard_map/ppermute | solution.py:37
Sparse Core Ops, SparseCore 0:
  74.3 68.6 all-gather.1
  170.0 114.4 reduce-scatter.1
where the time goes:
time: 309 us; the launch traced here: 307 us
  waiting for transfers between devices  193 us (62%)
  other arithmetic  71.1 us (23%)
  between operations  13.5 us (4%)
  matrix products  10.9 us (4%)
  local copies, waits for them, and re-layouts  9.95 us (3%)
  starting transfers between devices  8.76 us (3%)
    reduce_scatter x1, waiting for transfers between devices, shards(): lax.psum_scatter(dense_terms, 'frames', scatter_dimension=0, tiled=True)  115 us
    all_gather x1, waiting for transfers between devices, shards(): panel_piece = lax.all_gather(panel_values, 'slabs', axis=1, tiled=True)  62.8 us
    convert_element_type x1, other arithmetic, normalize(): jnp.where(mask == 1, jnp.zeros_like(scaled), scaled).astype(jnp.bfloat16)  31 us
    add x1, other arithmetic, box_total(): row_sums = row_sums + padded[:, offset:offset + row_count, :]  17.4 us
    scatter-add x1, other arithmetic, shards(): jax.ops.segment_sum(flat_terms, position, num_segments=owner_map.shape[1])  16 us
    dot_general x1, matrix products, shards(): product = jnp.dot(flat_rows, weights, preferred_element_type=jnp.float32)  10.9 us
    ppermute x1, waiting for transfers between devices, partner_2(): return lax.ppermute(block, axis, route)  10.5 us
  transfers between devices with their start and end apart: 5, of which 5 were waited for; matrix products, arithmetic and copies ran while one was open for 2% of the time, Pallas kernels for 0%

commit v1 on v0

v1 whole, which is shorter than its diff:
```python
import jax
import jax.numpy as jnp
from jax import lax
from jax.experimental import pallas as pl
from jax.experimental.pallas import tpu as pltpu
from jax.sharding import PartitionSpec as P

MESH = pl.DeviceIdType.MESH
F32 = jnp.float32
BF16 = jnp.bfloat16
I32 = jnp.int32

EPSILON = 1e-05
AREA = 81
SIDE = 4
FRAMES = 8
ROWS = 96
COLS = 1024
VOX = 1024
HALF = 512
PIX = 4096
BAND = 16
STEPS = ROWS // BAND
ENTRIES = FRAMES * BAND
PART = ENTRIES // SIDE
OWN = 128


def spread(v, amount, axis):
    return pltpu.roll(v, amount % v.shape[axis], axis)


def box_rows(v):
    n = v.shape[0] - 8
    s2 = v[0 : n + 7] + v[1 : n + 8]
    s4 = s2[0 : n + 5] + s2[2 : n + 7]
    s8 = s4[0:n] + s4[4 : n + 4]
    return s8 + v[8 : n + 8]


def box_cols(h):
    h = jnp.concatenate([h, jnp.zeros((h.shape[0], 128), F32)], axis=1)
    s2 = h + spread(h, -1, 1)
    s4 = s2 + spread(s2, -2, 1)
    total = s4 + spread(s4, 4, 1) + spread(h, -4, 1)
    return total[:, :COLS]


def kernel(
    px_hbm, mk_hbm, w_hbm, bl_ref, om_ref, mp_ref, out_ref,
    px, mk, w2, corr, x_all, acc, o_all, e_all, acc2, table, pos, pall, tgt,
    hs, hr, s2, r2, fsum, tot, sib_in, mir_in, own,
    ld_sem, hs_sem, hr_sem, ps_sem, pr_sem, zs_sem, zr_sem, ss_sem, sr_sem,
    as_sem, ar_sem, bs_sem, br_sem, fs_sem, fr_sem,
):
    me = lax.axis_index("frames")
    z = lax.axis_index("slabs")
    core = me % 2
    y = (me // 2) % SIDE
    x = me // (2 * SIDE)
    a = jnp.where(core == 0, x, y)
    b = jnp.where(core == 0, y, x)
    sib_a = jnp.where(core == 0, y, x)

    def dev(xx, yy, cc, zz):
        return {"frames": (xx * SIDE + yy) * 2 + cc, "slabs": zz}

    def along_a(i):
        aa = (a + i) % SIDE
        return dev(jnp.where(core == 0, aa, x), jnp.where(core == 0, y, aa), core, z)

    def along_b(i):
        bb = (b + i) % SIDE
        return dev(jnp.where(core == 0, x, bb), jnp.where(core == 0, bb, y), core, z)

    z_up = (z + 1) % SIDE
    z_down = (z + SIDE - 1) % SIDE
    z_far = (z + 2) % SIDE
    up = dev(x, y, core, z_up)
    down = dev(x, y, core, z_down)
    sib = dev(x, y, 1 - core, z)

    def remote(src, dst, ssem, rsem, to):
        return pltpu.make_async_remote_copy(
            src_ref=src, dst_ref=dst, send_sem=ssem, recv_sem=rsem, device_id=to, device_id_type=MESH
        )

    load_px = pltpu.make_async_copy(px_hbm, px.at[:, pl.ds(8, ROWS), :], ld_sem.at[0])
    load_mk = pltpu.make_async_copy(mk_hbm, mk, ld_sem.at[1])
    load_w = [
        pltpu.make_async_copy(w_hbm.at[0, :, pl.ds(h * HALF, HALF)], w2.at[h], ld_sem.at[2 + h]) for h in range(2)
    ]
    load_px.start()
    load_mk.start()
    for c in load_w:
        c.start()

    barrier = pltpu.get_barrier_semaphore()
    partners = [up, down, sib, dev(x, y, core, z_far), dev(x, y, 1 - core, z_far)]
    for i in range(1, SIDE):
        for cc in range(2):
            partners.append(dev((x + i) % SIDE, y, cc, z))
            partners.append(dev(x, (y + i) % SIDE, cc, z))
    for to in partners:
        pl.semaphore_signal(barrier, inc=1, device_id=to, device_id_type=MESH)
    pl.semaphore_wait(barrier, len(partners))

    halo_up = remote(hs.at[0], hr.at[0], hs_sem.at[0], hr_sem.at[0], up)
    halo_down = remote(hs.at[1], hr.at[1], hs_sem.at[1], hr_sem.at[1], down)

    def z_direct(t, kind):
        ref = x_all.at[t, z]
        return remote(ref, ref, zs_sem.at[t, kind], zr_sem.at[t, kind], (up, down)[kind])

    def z_forward(t, kind):
        ref = x_all.at[t, (z_down, z_up)[kind], :, pl.ds(kind * (PIX // 2), PIX // 2)]
        return remote(ref, ref, zs_sem.at[t, 2 + kind], zr_sem.at[t, 2 + kind], (up, down)[kind])

    def sib_copy(t):
        return remote(o_all.at[t], e_all.at[t, sib_a, core], ss_sem.at[t], sr_sem.at[t], sib)

    def a_direct(t, kind):
        ref = e_all.at[t, a]
        return remote(ref, ref, as_sem.at[t, kind], ar_sem.at[t, kind], along_a((1, SIDE - 1)[kind]))

    def a_forward(t, kind):
        ref = e_all.at[t, (a + (SIDE - 1, 1)[kind]) % SIDE, kind]
        return remote(ref, ref, as_sem.at[t, 2 + kind], ar_sem.at[t, 2 + kind], along_a((1, SIDE - 1)[kind]))

    def b_copy(i):
        return remote(s2.at[i - 1], r2.at[i - 1], bs_sem.at[i - 1], br_sem.at[i - 1], along_b(i))

    pos_copies = [remote(pos, pall.at[sib_a * 2 + core], ps_sem.at[0], pr_sem.at[sib_a * 2 + core], sib)]
    for i in range(1, SIDE):
        pos_copies.append(
            remote(pos, pall.at[x * 2 + core], ps_sem.at[2 * i - 1], pr_sem.at[x * 2 + core], dev((x + i) % SIDE, y, 0, z))
        )
        pos_copies.append(
            remote(pos, pall.at[y * 2 + core], ps_sem.at[2 * i], pr_sem.at[y * 2 + core], dev(x, (y + i) % SIDE, 1, z))
        )

    def find_positions():
        lane = lax.broadcasted_iota(I32, (1, STEPS * ENTRIES), 1)
        step = lane >> 7
        e = lane & (ENTRIES - 1)
        band = jnp.where(step < 4, step + 1, jnp.where(step == 4, 0, 5))
        panel = (e >> 5) * 24 + band * 4 + (e & 3)
        frame = (e >> 2) & 7
        pick = (lax.broadcasted_iota(I32, (96, STEPS * ENTRIES), 0) == panel).astype(F32).astype(BF16)
        listed = bl_ref[:, 0, :]
        high = (listed >> 6).astype(F32).astype(BF16)
        low = (listed & 63).astype(F32).astype(BF16)
        is_frame = lax.broadcasted_iota(I32, (FRAMES, STEPS * ENTRIES), 0) == frame

        def taken(v):
            got = jnp.dot(v, pick, preferred_element_type=F32)
            return jnp.sum(jnp.where(is_frame, got, 0.0), axis=0, keepdims=True)

        block = (taken(high) * 64.0 + taken(low)).astype(I32)
        for i in range(32):
            table[i : i + 1, :] = om_ref[:, i * 128 : (i + 1) * 128]
        entry = table[...]
        in_row = (lax.broadcasted_iota(I32, (128, STEPS * ENTRIES), 0) == (block & 127)).astype(F32).astype(BF16)
        row_hit = lax.broadcasted_iota(I32, (32, STEPS * ENTRIES), 0) == (block >> 7)

        def looked(v):
            got = jnp.dot(v.astype(F32).astype(BF16), in_row, preferred_element_type=F32)
            return jnp.sum(jnp.where(row_hit, got, 0.0), axis=0, keepdims=True)

        found = (looked(entry >> 6) * 64.0 + looked(entry & 63)).astype(I32)
        pos[...] = jnp.zeros_like(pos)
        for i in range(STEPS):
            pos[i : i + 1, :] = found[:, i * 128 : (i + 1) * 128]
        pall[a * 2 + core] = pos[...]

    def make_targets():
        for k in range(2 * SIDE):
            at = pall[k]
            owner = at >> 7
            to_a = jnp.where(core == 0, owner >> 3, (owner >> 1) & 3)
            to_b = jnp.where(core == 0, (owner >> 1) & 3, owner >> 3)
            row = ((to_b * 2 + (owner & 1)) << 7) + (at & 127)
            tgt[:, k * 128 : (k + 1) * 128] = jnp.where(to_a == a, row, -1)

    def fill_halo():
        for f in range(FRAMES):
            top = hr[0, f // 2, (f % 2) * 4 : (f % 2) * 4 + 4, :]
            px[f, 4:8, :] = jnp.where(z > 0, top, 0.0)
            bottom = hr[1, f // 2, (f % 2) * 4 : (f % 2) * 4 + 4, :]
            px[f, 8 + ROWS : 12 + ROWS, :] = jnp.where(z < SIDE - 1, bottom, 0.0)

    def normalize(t):
        band = jnp.where(t < 4, t + 1, jnp.where(t == 4, 0, 5))
        row0 = pl.multiple_of(band * BAND, BAND)

        @pl.loop(0, FRAMES)
        def _(f):
            rows = px[f, pl.ds(row0, 2 * BAND), :]
            v = rows[4:28]
            mean = box_cols(box_rows(v)) * (1.0 / AREA)
            square = box_cols(box_rows(v * v)) * (1.0 / AREA)
            var = square - mean * mean
            scaled = (rows[8:24] - mean) * lax.rsqrt(var + EPSILON)
            kept = jnp.where(mk[f, pl.ds(row0, BAND), :] == 1, 0.0, scaled)
            for v in range(8):
                corr[v, pl.ds(pl.multiple_of(f * BAND, BAND), BAND), :] = kept[:, v * 128 : (v + 1) * 128]

        for r in range(4):
            for v in range(8):
                at = slice(r * COLS + v * 128, r * COLS + (v + 1) * 128)
                x_all[t, z, :, at] = corr[v, pl.ds(r, PART, stride=4), :].astype(BF16)

    def multiply(t):
        for own_half in range(2):
            h = core if own_half else 1 - core
            acc[...] = jnp.zeros_like(acc)

            @pl.loop(0, 4)
            def _(kc):
                at = pl.ds(pl.multiple_of(kc * 1024, 1024), 1024)
                left = x_all[t, :, :, at].reshape(ENTRIES, 1024)
                acc[...] += jnp.dot(left, w2[h, at, :], preferred_element_type=F32)

            if own_half:
                e_all[t, a, core] = acc[...].astype(BF16)
            else:
                o_all[t] = acc[...].astype(BF16)
                sib_copy(t).start()

    def add_entries(t):
        row = tgt[pl.ds(t, 1), :]

        @pl.loop(0, SIDE)
        def _(blk):
            at = pl.ds(pl.multiple_of(blk * 256, 256), 256)
            hit = (lax.broadcasted_iota(I32, (256, 1024), 0) + blk * 256) == row
            terms = e_all[t].reshape(1024, HALF)
            acc2[at, :] += jnp.dot(hit.astype(F32).astype(BF16), terms, preferred_element_type=F32)

    acc2[...] = jnp.zeros_like(acc2)
    load_px.wait()
    for f in range(FRAMES):
        at = slice((f % 2) * 4, (f % 2) * 4 + 4)
        hs[0, f // 2, at, :] = px[f, 4 + ROWS : 8 + ROWS, :]
        hs[1, f // 2, at, :] = px[f, 8:12, :]
    halo_up.start()
    halo_down.start()
    load_mk.wait()

    @pl.loop(0, STEPS + 4)
    def _(t):
        @pl.when(t == 4)
        def _():
            halo_up.wait_recv()
            halo_down.wait_recv()
            fill_halo()

        @pl.when(t < STEPS)
        def _():
            normalize(t)
            z_direct(t, 0).start()
            z_direct(t, 1).start()

        @pl.when(t == 0)
        def _():
            find_positions()
            for c in pos_copies:
                c.start()

        @pl.when((t >= 1) & (t < STEPS + 1))
        def _():
            for kind in range(2):
                z_direct(t - 1, kind).wait_recv()
                z_forward(t - 1, kind).start()

        @pl.when((t >= 3) & (t < STEPS + 3))
        def _():
            for kind in range(2):
                a_direct(t - 3, kind).wait_recv()
                a_forward(t - 3, kind).start()

        @pl.when(t == 2)
        def _():
            for c in load_w:
                c.wait()

        @pl.when((t >= 2) & (t < STEPS + 2))
        def _():
            for kind in range(2):
                z_forward(t - 2, kind).wait_recv()
            multiply(t - 2)

        @pl.when(t == 4)
        def _():
            def arrived(k):
                remote(pos, pall.at[k], ps_sem.at[0], pr_sem.at[k], sib).wait_recv()

            arrived(a * 2 + 1 - core)
            for i in range(1, SIDE):
                for g in range(2):
                    arrived(((a + i) % SIDE) * 2 + g)
            make_targets()

        @pl.when(t >= 4)
        def _():
            for kind in range(2):
                a_forward(t - 4, kind).wait_recv()
            add_entries(t - 4)

        @pl.when((t >= 2) & (t < STEPS + 2))
        def _():
            sib_copy(t - 2).wait_recv()
            a_direct(t - 2, 0).start()
            a_direct(t - 2, 1).start()

    for i in (2, 1, 3):
        at = pl.ds(pl.multiple_of(((b + i) % SIDE) * 256, 256), 256)
        s2[i - 1] = acc2[at, :].astype(BF16)
        b_copy(i).start()
    tot[...] = acc2[pl.ds(pl.multiple_of(b * 256, 256), 256), :]
    for i in (1, 3, 2):
        b_copy(i).wait_recv()
        tot[...] += r2[i - 1].astype(F32)
    for cc in range(2):
        fsum[cc] = tot[cc * OWN : (cc + 1) * OWN, :].astype(BF16)
    last = [
        remote(fsum.at[0], mir_in.at[core], fs_sem.at[0], fr_sem.at[core], dev(x, y, 0, z_far)),
        remote(fsum.at[1], mir_in.at[core], fs_sem.at[1], fr_sem.at[core], dev(x, y, 1, z_far)),
        remote(fsum.at[1 - core], sib_in, fs_sem.at[2], fr_sem.at[2], sib),
    ]
    for c in last:
        c.start()
    own[core] = tot[pl.ds(pl.multiple_of(core * OWN, OWN), OWN), :]
    pick = (lax.broadcasted_iota(I32, (OWN, OWN), 0) == mp_ref[...]).astype(F32).astype(BF16)
    flip = (
        lax.broadcasted_iota(I32, (OWN, OWN), 0) + lax.broadcasted_iota(I32, (OWN, OWN), 1) == OWN - 1
    ).astype(F32).astype(BF16)
    last[2].wait_recv()
    own[1 - core] = sib_in[...].astype(F32)
    for h in range(2):
        remote(fsum.at[0], mir_in.at[h], fs_sem.at[0], fr_sem.at[h], dev(x, y, 0, z_far)).wait_recv()
    for h in range(2):
        rows = lax.dot_general(pick, mir_in[1 - h], (((0,), (0,)), ((), ())), preferred_element_type=F32).astype(BF16)
        for v in range(4):
            turned = jnp.dot(rows[:, (3 - v) * OWN : (4 - v) * OWN], flip, preferred_element_type=F32)
            out_ref[0, :, h * HALF + v * OWN : h * HALF + (v + 1) * OWN] = 0.5 * (
                own[h, :, v * OWN : (v + 1) * OWN] + turned
            )

    halo_up.wait_send()
    halo_down.wait_send()
    for c in pos_copies:
        c.wait_send()

    @pl.loop(0, STEPS)
    def _(t):
        for kind in range(2):
            z_direct(t, kind).wait_send()
            z_forward(t, kind).wait_send()
            a_direct(t, kind).wait_send()
            a_forward(t, kind).wait_send()
        sib_copy(t).wait_send()

    for i in range(1, SIDE):
        b_copy(i).wait_send()
    for c in last:
        c.wait_send()


def shards(frame_pixels, bragg_mask, interp, block_list, owner_map, mirror_pair):
    vmem = pl.BlockSpec(memory_space=pltpu.VMEM)
    hbm = pl.BlockSpec(memory_space=pl.ANY)
    dma = pltpu.SemaphoreType.DMA
    return pl.pallas_call(
        kernel,
        out_shape=jax.ShapeDtypeStruct((1, OWN, VOX), F32),
        in_specs=[hbm, hbm, hbm, vmem, vmem, vmem],
        out_specs=vmem,
        scratch_shapes=[
            pltpu.VMEM((FRAMES, ROWS + 16, COLS), F32),
            pltpu.VMEM((FRAMES, ROWS, COLS), I32),
            pltpu.VMEM((2, PIX, HALF), BF16),
            pltpu.VMEM((8, ENTRIES, 128), F32),
            pltpu.VMEM((STEPS, SIDE, PART, PIX), BF16),
            pltpu.VMEM((ENTRIES, HALF), F32),
            pltpu.VMEM((STEPS, ENTRIES, HALF), BF16),
            pltpu.VMEM((STEPS, SIDE, 2, ENTRIES, HALF), BF16),
            pltpu.VMEM((1024, HALF), F32),
            pltpu.VMEM((32, 128), I32),
            pltpu.VMEM((8, 128), I32),
            pltpu.VMEM((2 * SIDE, 8, 128), I32),
            pltpu.VMEM((8, 1024), I32),
            pltpu.VMEM((2, FRAMES // 2, 8, COLS), F32),
            pltpu.VMEM((2, FRAMES // 2, 8, COLS), F32),
            pltpu.VMEM((3, 256, HALF), BF16),
            pltpu.VMEM((3, 256, HALF), BF16),
            pltpu.VMEM((2, OWN, HALF), BF16),
            pltpu.VMEM((256, HALF), F32),
            pltpu.VMEM((OWN, HALF), BF16),
            pltpu.VMEM((2, OWN, HALF), BF16),
            pltpu.VMEM((2, OWN, HALF), F32),
            dma((4,)),
            dma((2,)),
            dma((2,)),
            dma((7,)),
            dma((8,)),
            dma((STEPS, 4)),
            dma((STEPS, 4)),
            dma((STEPS,)),
            dma((STEPS,)),
            dma((STEPS, 4)),
            dma((STEPS, 4)),
            dma((3,)),
            dma((3,)),
            dma((3,)),
            dma((3,)),
        ],
        compiler_params=pltpu.CompilerParams(
            collective_id=0, has_side_effects=True, vmem_limit_bytes=60 * 1024 * 1024
        ),
    )(frame_pixels, bragg_mask, interp, block_list, owner_map, mirror_pair)


def solution(mesh):
    return jax.shard_map(
        shards,
        mesh=mesh,
        in_specs=(
            P("frames", "slabs", None),
            P("frames", "slabs", None),
            P("slabs", None, None),
            P("frames", "slabs", None),
            P("slabs", None),
            P("slabs", None),
        ),
        out_specs=P("slabs", "frames", None),
        check_vma=False,
    )
```

time: 309 us -> 113 us (0.37)
  waiting for transfers between devices: 193 us -> 0 us
  Pallas kernels: 0 us -> 110 us
  other arithmetic: 71.1 us -> 0 us
  between operations: 13.5 us -> 0.01 us
  matrix products: 10.9 us -> 0 us
  starting transfers between devices: 8.76 us -> 0 us
  local copies, waits for them, and re-layouts: 9.95 us -> 1.89 us
    reduce_scatter x1 -> x0, waiting for transfers between devices: 115 us -> none  [shards(): lax.psum_scatter(dense_terms, 'frames', scatter_dimension=0, tiled=True)]
    pallas_call x0 -> x1, Pallas kernels: none -> 110 us  [shards(): pl.pallas_call(kernel, out_shape=jax.ShapeDtypeStruct((1, OWN, VOX), F32)...]
    all_gather x1 -> x0, waiting for transfers between devices: 62.8 us -> none  [shards(): panel_piece = lax.all_gather(panel_values, 'slabs', axis=1, tiled=True)]
    convert_element_type x1 -> x0, other arithmetic: 31 us -> none  [normalize(): jnp.where(mask == 1, jnp.zeros_like(scaled), scaled).astype(jnp.bfloat16)]
    add x1 -> x0, other arithmetic: 17.4 us -> none  [box_total(): row_sums = row_sums + padded[:, offset:offset + row_count, :]]
    scatter-add x1 -> x0, other arithmetic: 16 us -> none  [shards(): jax.ops.segment_sum(flat_terms, position, num_segments=owner_map.shape[1])]
    ppermute x3 -> x0, waiting for transfers between devices: 15.5 us -> none  [the longest x1 10.5 us: partner_2(): return lax.ppermute(block, axis, route)]
    dot_general x1 -> x0, matrix products: 10.9 us -> none  [shards(): product = jnp.dot(flat_rows, weights, preferred_element_type=jnp.float32)]
  transfers between devices with their start and end apart: 5 -> 0, of which waited for: 5 -> 0; matrix products, arithmetic and copies ran while one was open for 2% -> 0% of each run, Pallas kernels for 0% -> 0%
where the time goes in v1:
time: 113 us; the launch traced here: 112 us
  Pallas kernels  110 us (97%)
  local copies, waits for them, and re-layouts  1.89 us (2%)
    pallas_call x1, Pallas kernels, shards(): pl.pallas_call(kernel, out_shape=jax.ShapeDtypeStruct((1, OWN, VOX), F32)...  110 us

profile of v1, /device:TPU:1, one launch (start us, length us, event | category | flops | bytes accessed | tf_op | source)
XLA Modules:
  0.0 112.4 jit_solution(11356388345299080898)
XLA Ops:
  0.0 110.5 %shard_map.64 = f32[1,128,1024]{2,1,0:T(8,128)} custom-call(f32[8,96,1024]{2,1,0:T(8,128)} %px_hbm.1, s32[8,96,1024]{2,1,0:T(8,128)} %mk_hbm.1, bf16[1,4096,1024]{2,1,0:T(8,128)(2,1)} %w_hbm.1, s32[8,1,96]{2,1,0:T(1,128)} %bl_ref.1, s32[1,4096]{1,0:T(1,128)} %om_ref.1, s32[1,128]{1,0:T(1,128)} %mp_ref.1), custom_call_target="tpu_custom_call" | custom-call | tf_op jit(solution)/shard_map/pallas_call | solution.py:374
  110.5 1.9 %copy.8 = f32[1,128,1024]{2,1,0:T(8,128)} copy(f32[1,128,1024]{2,1,0:T(8,128)} %shard_map.64) | data formatting | bytes 1048576

commit v2 on v1

v2 whole, which is shorter than its diff:
```python
import jax
import jax.numpy as jnp
from jax import lax
from jax.experimental import pallas as pl
from jax.experimental.pallas import tpu as pltpu
from jax.sharding import PartitionSpec as P

MESH = pl.DeviceIdType.MESH
F32 = jnp.float32
BF16 = jnp.bfloat16
I32 = jnp.int32

EPSILON = 1e-05
AREA = 81
SIDE = 4
FRAMES = 8
ROWS = 96
COLS = 1024
VOX = 1024
HALF = 512
QUART = 256
FIRST_ROWS = 56
PIX = 4096
BAND = 16
STEPS = ROWS // BAND
PART = FRAMES * BAND // 4
ENTRIES = 3 * PART
UNITS = STEPS + STEPS // 3
OWN = 128


def spread(v, amount, axis):
    return pltpu.roll(v, amount % v.shape[axis], axis)


def box_rows(v):
    n = v.shape[0] - 8
    s2 = v[0 : n + 7] + v[1 : n + 8]
    s4 = s2[0 : n + 5] + s2[2 : n + 7]
    s8 = s4[0:n] + s4[4 : n + 4]
    return s8 + v[8 : n + 8]


def box_cols(h):
    h = jnp.concatenate([h, jnp.zeros((h.shape[0], 128), F32)], axis=1)
    s2 = h + spread(h, -1, 1)
    s4 = s2 + spread(s2, -2, 1)
    total = s4 + spread(s4, 4, 1) + spread(h, -4, 1)
    return total[:, :COLS]


def kernel(
    px_hbm, mk_hbm, w_hbm, bl_ref, om_ref, mp_ref, out_ref,
    px, mk, w4, corr, x_all, acc, o_all, e_all, acc2, hits, table, pos, pall, tgt,
    hs, hr, s2, r2, fsum, tot, mir_in, own,
    ld_sem, lw_sem, hs_sem, hr_sem, ps_sem, pr_sem, zs_sem, zr_sem,
    as_sem, ar_sem, bs_sem, br_sem, fs_sem, fr_sem,
):
    me = lax.axis_index("frames")
    z = lax.axis_index("slabs")
    core = me % 2
    y = (me // 2) % SIDE
    x = me // (2 * SIDE)
    a = jnp.where(core == 0, x, y)
    b = jnp.where(core == 0, y, x)
    mine = a * 2 + core

    def dev(xx, yy, cc, zz):
        return {"frames": (xx * SIDE + yy) * 2 + cc, "slabs": zz}

    def along_b(i):
        bb = (b + i) % SIDE
        return dev(jnp.where(core == 0, x, bb), jnp.where(core == 0, bb, y), core, z)

    z_up = (z + 1) % SIDE
    z_down = (z + SIDE - 1) % SIDE
    z_far = (z + 2) % SIDE
    up = dev(x, y, core, z_up)
    down = dev(x, y, core, z_down)
    sib = dev(x, y, 1 - core, z)

    def along_a(i):
        aa = (a + i) % SIDE
        return dev(jnp.where(core == 0, aa, x), jnp.where(core == 0, y, aa), core, z)

    def along_other(i):
        aa = (b + i) % SIDE
        return dev(jnp.where(core == 0, x, aa), jnp.where(core == 0, aa, y), 1 - core, z)

    def remote(src, dst, ssem, rsem, to):
        return pltpu.make_async_remote_copy(
            src_ref=src, dst_ref=dst, send_sem=ssem, recv_sem=rsem, device_id=to, device_id_type=MESH
        )

    first = FIRST_ROWS
    loads = [
        pltpu.make_async_copy(px_hbm.at[:, pl.ds(0, first), :], px.at[:, pl.ds(8, first), :], ld_sem.at[0]),
        pltpu.make_async_copy(mk_hbm.at[:, pl.ds(0, first), :], mk.at[:, pl.ds(0, first), :], ld_sem.at[1]),
        pltpu.make_async_copy(
            px_hbm.at[:, pl.ds(first, ROWS - first), :], px.at[:, pl.ds(8 + first, ROWS - first), :], ld_sem.at[2]
        ),
        pltpu.make_async_copy(
            mk_hbm.at[:, pl.ds(first, ROWS - first), :], mk.at[:, pl.ds(first, ROWS - first), :], ld_sem.at[3]
        ),
    ]
    load_w = [
        pltpu.make_async_copy(w_hbm.at[0, :, pl.ds(i * QUART, QUART)], w4.at[i], lw_sem.at[i]) for i in range(4)
    ]
    for c in loads:
        c.start()

    barrier = pltpu.get_barrier_semaphore()
    partners = [up, down, sib, dev(x, y, core, z_far), dev(x, y, 1 - core, z_far)]
    for i in range(1, SIDE):
        for cc in range(2):
            partners.append(dev((x + i) % SIDE, y, cc, z))
            partners.append(dev(x, (y + i) % SIDE, cc, z))
    for to in partners:
        pl.semaphore_signal(barrier, inc=1, device_id=to, device_id_type=MESH)

    halo_up = remote(hs.at[0], hr.at[0], hs_sem.at[0], hr_sem.at[0], up)
    halo_down = remote(hs.at[1], hr.at[1], hs_sem.at[1], hr_sem.at[1], down)

    def z_direct(t, kind):
        return remote(x_all.at[t, 0], x_all.at[t, 1 + kind], zs_sem.at[t, kind], zr_sem.at[t, kind], (up, down)[kind])

    def z_forward(t, kind):
        at = pl.ds(kind * (PIX // 2), PIX // 2)
        src, dst = x_all.at[t, 1 + kind, :, at], x_all.at[STEPS + t // 3, t % 3, :, at]
        return remote(src, dst, zs_sem.at[t, 2 + kind], zr_sem.at[t, 2 + kind], (up, down)[kind])

    def entry_copies(t, q):
        copies = []
        for i in range(SIDE):
            slot = b * 2 + core
            copies.append(
                remote(o_all.at[t, q], e_all.at[t, q, slot], as_sem.at[t, q, i], ar_sem.at[t, q, slot], along_other(i))
            )
        for i in range(1, SIDE):
            ref = e_all.at[t, q, mine]
            copies.append(remote(ref, ref, as_sem.at[t, q, 3 + i], ar_sem.at[t, q, mine], along_a(i)))
        return copies

    def others():
        return [a * 2 + 1 - core] + [((a + i) % SIDE) * 2 + g for i in range(1, SIDE) for g in range(2)]

    def entries_arrived(t, q):
        for k in others():
            ref = e_all.at[t, q, k]
            remote(ref, ref, as_sem.at[t, q, 0], ar_sem.at[t, q, k], sib).wait_recv()

    def b_copy(i, q):
        return remote(s2.at[q, i - 1], r2.at[q, i - 1], bs_sem.at[q, i - 1], br_sem.at[q, i - 1], along_b(i))

    def last_copies(q):
        ref = tot.at[q, pl.ds(pl.multiple_of((1 - core) * OWN, OWN), OWN)]
        return [
            remote(fsum.at[q, 0], mir_in.at[core, q], fs_sem.at[q, 0], fr_sem.at[q, core], dev(x, y, 0, z_far)),
            remote(fsum.at[q, 1], mir_in.at[core, q], fs_sem.at[q, 1], fr_sem.at[q, core], dev(x, y, 1, z_far)),
            remote(ref, own.at[core, q], fs_sem.at[q, 2], fr_sem.at[q, 2], sib),
        ]

    pos_copies = []
    for i in range(SIDE):
        slot = b * 2 + core
        pos_copies.append(remote(pos, pall.at[slot], ps_sem.at[i], pr_sem.at[slot], along_other(i)))
    for i in range(1, SIDE):
        pos_copies.append(remote(pos, pall.at[mine], ps_sem.at[3 + i], pr_sem.at[mine], along_a(i)))

    def find_positions():
        lane = lax.broadcasted_iota(I32, (1, UNITS * 128), 1)
        unit = lane >> 7
        third = (lane >> 5) & 3
        near = unit < STEPS
        step = jnp.where(near, unit, (unit - STEPS) * 3 + third)
        band = jnp.where(step < 4, step + 1, jnp.where(step == 4, 0, 5))
        apart = jnp.where(near, jnp.where(third == 0, 0, jnp.where(third == 1, 3, 1)), 2)
        panel = ((z + apart) & 3) * 24 + band * 4 + (lane & 3)
        frame = (lane >> 2) & 7
        pick = (lax.broadcasted_iota(I32, (96, UNITS * 128), 0) == panel).astype(F32).astype(BF16)
        listed = bl_ref[:, 0, :]
        high = (listed >> 6).astype(F32).astype(BF16)
        low = (listed & 63).astype(F32).astype(BF16)
        is_frame = lax.broadcasted_iota(I32, (FRAMES, UNITS * 128), 0) == frame

        def taken(v):
            got = jnp.dot(v, pick, preferred_element_type=F32)
            return jnp.sum(jnp.where(is_frame, got, 0.0), axis=0, keepdims=True)

        block = (taken(high) * 64.0 + taken(low)).astype(I32)
        for i in range(32):
            table[i : i + 1, :] = om_ref[:, i * 128 : (i + 1) * 128]
        entry = table[...]
        in_row = (lax.broadcasted_iota(I32, (128, UNITS * 128), 0) == (block & 127)).astype(F32).astype(BF16)
        row_hit = lax.broadcasted_iota(I32, (32, UNITS * 128), 0) == (block >> 7)

        def looked(v):
            got = jnp.dot(v.astype(F32).astype(BF16), in_row, preferred_element_type=F32)
            return jnp.sum(jnp.where(row_hit, got, 0.0), axis=0, keepdims=True)

        found = (looked(entry >> 6) * 64.0 + looked(entry & 63)).astype(I32)
        for i in range(UNITS):
            pos[i : i + 1, :] = found[:, i * 128 : (i + 1) * 128]
        pall[mine] = pos[...]

    def make_targets():
        for k in range(2 * SIDE):
            at = pall[k]
            owner = at >> 7
            to_a = jnp.where(core == 0, owner >> 3, (owner >> 1) & 3)
            to_b = jnp.where(core == 0, (owner >> 1) & 3, owner >> 3)
            row = ((to_b * 2 + (owner & 1)) << 7) + (at & 127)
            tgt[:, k * ENTRIES : (k + 1) * ENTRIES] = jnp.where(to_a == a, row, -1)[:, :ENTRIES]

    def send_halo():
        for f in range(FRAMES):
            at = slice((f % 2) * 4, (f % 2) * 4 + 4)
            hs[0, f // 2, at, :] = px[f, 4 + ROWS : 8 + ROWS, :]
            hs[1, f // 2, at, :] = px[f, 8:12, :]
        halo_up.start()
        halo_down.start()

    def fill_halo():
        for f in range(FRAMES):
            top = hr[0, f // 2, (f % 2) * 4 : (f % 2) * 4 + 4, :]
            px[f, 4:8, :] = jnp.where(z > 0, top, 0.0)
            bottom = hr[1, f // 2, (f % 2) * 4 : (f % 2) * 4 + 4, :]
            px[f, 8 + ROWS : 12 + ROWS, :] = jnp.where(z < SIDE - 1, bottom, 0.0)

    def normalize(t):
        band = jnp.where(t < 4, t + 1, jnp.where(t == 4, 0, 5))
        row0 = pl.multiple_of(band * BAND, BAND)

        @pl.loop(0, FRAMES)
        def _(f):
            rows = px[f, pl.ds(row0, 2 * BAND), :]
            v = rows[4:28]
            mean = box_cols(box_rows(v)) * (1.0 / AREA)
            square = box_cols(box_rows(v * v)) * (1.0 / AREA)
            var = square - mean * mean
            scaled = (rows[8:24] - mean) * lax.rsqrt(var + EPSILON)
            kept = jnp.where(mk[f, pl.ds(row0, BAND), :] == 1, 0.0, scaled)
            for v in range(8):
                corr[v, pl.ds(pl.multiple_of(f * BAND, BAND), BAND), :] = kept[:, v * 128 : (v + 1) * 128]

        for r in range(4):
            for v in range(8):
                at = slice(r * COLS + v * 128, r * COLS + (v + 1) * 128)
                x_all[t, 0, :, at] = corr[v, pl.ds(r, PART, stride=4), :].astype(BF16)

    def z_start(t):
        for kind in range(2):
            z_direct(t, kind).start()

    def multiply(t):
        for q in range(2):
            for own_half in range(2):
                h = core if own_half else 1 - core
                part = jnp.dot(
                    x_all[t].reshape(ENTRIES, PIX), w4[h * 2 + q], preferred_element_type=F32
                ).astype(BF16)
                if own_half:
                    e_all[t, q, mine] = part
                else:
                    o_all[t, q] = part
            for c in entry_copies(t, q):
                c.start()

    def make_hits(t):
        row = tgt[pl.ds(t, 1), :]

        @pl.loop(0, SIDE)
        def _(blk):
            hit = (lax.broadcasted_iota(I32, (256, 2 * SIDE * ENTRIES), 0) + blk * 256) == row
            hits[blk] = hit.astype(F32).astype(BF16)

    def add_entries(t, q, blk):
        acc2[q, blk] += jnp.dot(
            hits[blk], e_all[t, q].reshape(2 * SIDE * ENTRIES, QUART), preferred_element_type=F32
        )

    def add_all(t):
        make_hits(t)
        for q in range(2):
            entries_arrived(t, q)
            sums = jnp.dot(
                hits[...].reshape(SIDE * 256, 2 * SIDE * ENTRIES),
                e_all[t, q].reshape(2 * SIDE * ENTRIES, QUART),
                preferred_element_type=F32,
            )
            acc2[q] += sums.reshape(SIDE, 256, QUART)

    acc2[...] = jnp.zeros_like(acc2)
    loads[0].wait()
    loads[1].wait()
    for c in load_w:
        c.start()

    @pl.loop(0, 2)
    def _(t):
        normalize(t)

    pl.semaphore_wait(barrier, len(partners))
    z_start(0)
    z_start(1)
    loads[2].wait()
    loads[3].wait()
    send_halo()
    find_positions()
    for c in pos_copies:
        c.start()

    @pl.loop(0, STEPS)
    def _(t):
        @pl.when(t == 2)
        def _():
            halo_up.wait_recv()
            halo_down.wait_recv()
            fill_halo()

        @pl.when(t < STEPS - 2)
        def _():
            normalize(t + 2)
            z_start(t + 2)

        for kind in range(2):
            z_direct(t, kind).wait_recv()
            z_forward(t, kind).start()

        @pl.when(t == 0)
        def _():
            for c in load_w:
                c.wait()

        multiply(t)

        @pl.when(t == 1)
        def _():
            for k in others():
                remote(pos, pall.at[k], ps_sem.at[0], pr_sem.at[k], sib).wait_recv()
            make_targets()

        @pl.when(t >= 1)
        def _():
            add_all(t - 1)

    end = UNITS - 1

    def far(u):
        for i in range(3):
            for kind in range(2):
                z_forward((u - STEPS) * 3 + i, kind).wait_recv()

    far(end - 1)
    multiply(end - 1)
    add_all(end - 2)
    far(end)
    multiply(end)
    add_all(end - 1)
    make_hits(end)

    for q in range(2):
        entries_arrived(end, q)
        for i in (2, 1, 3, 0):
            blk = (b + i) % SIDE
            add_entries(end, q, blk)
            if i:
                s2[q, i - 1] = acc2[q, blk].astype(BF16)
                b_copy(i, q).start()
    for q in range(2):
        for i in range(1, SIDE):
            b_copy(i, q).wait_recv()
        total = acc2[q, b] + (r2[q, 0].astype(F32) + r2[q, 1].astype(F32) + r2[q, 2].astype(F32))
        tot[q] = total
        for cc in range(2):
            fsum[q, cc] = total[cc * OWN : (cc + 1) * OWN, :].astype(BF16)
        for c in last_copies(q):
            c.start()
        own[core, q] = tot[q, pl.ds(pl.multiple_of(core * OWN, OWN), OWN), :]
    pick = (lax.broadcasted_iota(I32, (OWN, OWN), 0) == mp_ref[...]).astype(F32).astype(BF16)
    flip = (
        lax.broadcasted_iota(I32, (OWN, OWN), 0) + lax.broadcasted_iota(I32, (OWN, OWN), 1) == OWN - 1
    ).astype(F32).astype(BF16)
    for q in range(2):
        remote(own.at[0, q], own.at[0, q], fs_sem.at[q, 2], fr_sem.at[q, 2], sib).wait_recv()
        for h in range(2):
            ref = mir_in.at[h, q]
            remote(ref, ref, fs_sem.at[q, 0], fr_sem.at[q, h], dev(x, y, 0, z_far)).wait_recv()
        for h in range(2):
            rows = lax.dot_general(
                pick, mir_in[1 - h, q], (((0,), (0,)), ((), ())), preferred_element_type=F32
            ).astype(BF16)
            for v in range(2):
                turned = jnp.dot(rows[:, (1 - v) * OWN : (2 - v) * OWN], flip, preferred_element_type=F32)
                at = h * HALF + (1 - q) * QUART + v * OWN
                out_ref[0, :, at : at + OWN] = turned
    for q in range(2):
        for h in range(2):
            at = slice(h * HALF + q * QUART, h * HALF + (q + 1) * QUART)
            out_ref[0, :, at] = 0.5 * (own[h, q] + out_ref[0, :, at])

    halo_up.wait_send()
    halo_down.wait_send()
    for c in pos_copies:
        c.wait_send()

    @pl.loop(0, STEPS)
    def _(t):
        for kind in range(2):
            z_direct(t, kind).wait_send()
            z_forward(t, kind).wait_send()

    @pl.loop(0, UNITS)
    def _(t):
        for q in range(2):
            for c in entry_copies(t, q):
                c.wait_send()

    for q in range(2):
        for i in range(1, SIDE):
            b_copy(i, q).wait_send()
        for c in last_copies(q):
            c.wait_send()


def shards(frame_pixels, bragg_mask, interp, block_list, owner_map, mirror_pair):
    vmem = pl.BlockSpec(memory_space=pltpu.VMEM)
    hbm = pl.BlockSpec(memory_space=pl.ANY)
    dma = pltpu.SemaphoreType.DMA
    return pl.pallas_call(
        kernel,
        out_shape=jax.ShapeDtypeStruct((1, OWN, VOX), F32),
        in_specs=[hbm, hbm, hbm, vmem, vmem, vmem],
        out_specs=vmem,
        scratch_shapes=[
            pltpu.VMEM((FRAMES, ROWS + 16, COLS), F32),
            pltpu.VMEM((FRAMES, ROWS, COLS), I32),
            pltpu.VMEM((4, PIX, QUART), BF16),
            pltpu.VMEM((8, FRAMES * BAND, 128), F32),
            pltpu.VMEM((UNITS, 3, PART, PIX), BF16),
            pltpu.VMEM((ENTRIES, QUART), F32),
            pltpu.VMEM((UNITS, 2, ENTRIES, QUART), BF16),
            pltpu.VMEM((UNITS, 2, 2 * SIDE, ENTRIES, QUART), BF16),
            pltpu.VMEM((2, SIDE, 256, QUART), F32),
            pltpu.VMEM((SIDE, 256, 2 * SIDE * ENTRIES), BF16),
            pltpu.VMEM((32, 128), I32),
            pltpu.VMEM((8, 128), I32),
            pltpu.VMEM((2 * SIDE, 8, 128), I32),
            pltpu.VMEM((8, 2 * SIDE * ENTRIES), I32),
            pltpu.VMEM((2, FRAMES // 2, 8, COLS), F32),
            pltpu.VMEM((2, FRAMES // 2, 8, COLS), F32),
            pltpu.VMEM((2, 3, 256, QUART), BF16),
            pltpu.VMEM((2, 3, 256, QUART), BF16),
            pltpu.VMEM((2, 2, OWN, QUART), BF16),
            pltpu.VMEM((2, 256, QUART), F32),
            pltpu.VMEM((2, 2, OWN, QUART), BF16),
            pltpu.VMEM((2, 2, OWN, QUART), F32),
            dma((4,)),
            dma((4,)),
            dma((2,)),
            dma((2,)),
            dma((7,)),
            dma((8,)),
            dma((STEPS, 4)),
            dma((STEPS, 4)),
            dma((UNITS, 2, 7)),
            dma((UNITS, 2, 8)),
            dma((2, 3)),
            dma((2, 3)),
            dma((2, 3)),
            dma((2, 3)),
        ],
        compiler_params=pltpu.CompilerParams(
            collective_id=0, has_side_effects=True, vmem_limit_bytes=60 * 1024 * 1024
        ),
    )(frame_pixels, bragg_mask, interp, block_list, owner_map, mirror_pair)


def solution(mesh):
    return jax.shard_map(
        shards,
        mesh=mesh,
        in_specs=(
            P("frames", "slabs", None),
            P("frames", "slabs", None),
            P("slabs", None, None),
            P("frames", "slabs", None),
            P("slabs", None),
            P("slabs", None),
        ),
        out_specs=P("slabs", "frames", None),
        check_vma=False,
    )
```

time: 113 us -> 96.4 us (0.85)
  Pallas kernels: 110 us -> 94.3 us
    pallas_call x1, Pallas kernels: 110 us -> 94.3 us  [shards(): pl.pallas_call(kernel, out_shape=jax.ShapeDtypeStruct((1, OWN, VOX), F32)...]
where the time goes in v2:
time: 96.4 us; the launch traced here: 96.2 us
  Pallas kernels  94.3 us (98%)
  local copies, waits for them, and re-layouts  1.89 us (2%)
    pallas_call x1, Pallas kernels, shards(): pl.pallas_call(kernel, out_shape=jax.ShapeDtypeStruct((1, OWN, VOX), F32)...  94.3 us

profile of v2, /device:TPU:1, one launch (start us, length us, event | category | flops | bytes accessed | tf_op | source)
XLA Modules:
  0.0 96.2 jit_solution(12759528281562957461)
XLA Ops:
  0.0 94.3 %shard_map.64 = f32[1,128,1024]{2,1,0:T(8,128)} custom-call(f32[8,96,1024]{2,1,0:T(8,128)} %px_hbm.1, s32[8,96,1024]{2,1,0:T(8,128)} %mk_hbm.1, bf16[1,4096,1024]{2,1,0:T(8,128)(2,1)} %w_hbm.1, s32[8,1,96]{2,1,0:T(1,128)} %bl_ref.1, s32[1,4096]{1,0:T(1,128)} %om_ref.1, s32[1,128]{1,0:T(1,128)} %mp_ref.1), custom_call_target="tpu_custom_call" | custom-call | tf_op jit(solution)/shard_map/pallas_call | solution.py:430
  94.3 1.9 %copy.8 = f32[1,128,1024]{2,1,0:T(8,128)} copy(f32[1,128,1024]{2,1,0:T(8,128)} %shard_map.64) | data formatting | bytes 1048576

commit v3 on v2

--- a/solution.py
+++ b/solution.py
@@ -19,7 +19,7 @@
 VOX = 1024
 HALF = 512
 QUART = 256
-FIRST_ROWS = 56
+FIRST_ROWS = 40
 PIX = 4096
 BAND = 16
 STEPS = ROWS // BAND
@@ -27,6 +27,9 @@
 ENTRIES = 3 * PART
 UNITS = STEPS + STEPS // 3
 OWN = 128
+ALL = pl.ds(0, ENTRIES)
+EARLY = pl.ds(0, 2 * PART)
+LATE = pl.ds(2 * PART, PART)
 
 
 def spread(v, amount, axis):
@@ -129,25 +132,26 @@
         src, dst = x_all.at[t, 1 + kind, :, at], x_all.at[STEPS + t // 3, t % 3, :, at]
         return remote(src, dst, zs_sem.at[t, 2 + kind], zr_sem.at[t, 2 + kind], (up, down)[kind])
 
-    def entry_copies(t, q):
+    def entry_copies(n, t, at, q=None):
+        cols, m = (pl.ds(0, 2), 0) if q is None else (pl.ds(q, 1), q)
+        slot = b * 2 + core
         copies = []
         for i in range(SIDE):
-            slot = b * 2 + core
-            copies.append(
-                remote(o_all.at[t, q], e_all.at[t, q, slot], as_sem.at[t, q, i], ar_sem.at[t, q, slot], along_other(i))
-            )
+            src, dst = o_all.at[t, cols, at], e_all.at[t, cols, slot, at]
+            copies.append(remote(src, dst, as_sem.at[n, m, i], ar_sem.at[n, m, slot], along_other(i)))
         for i in range(1, SIDE):
-            ref = e_all.at[t, q, mine]
-            copies.append(remote(ref, ref, as_sem.at[t, q, 3 + i], ar_sem.at[t, q, mine], along_a(i)))
+            ref = e_all.at[t, cols, mine, at]
+            copies.append(remote(ref, ref, as_sem.at[n, m, 3 + i], ar_sem.at[n, m, mine], along_a(i)))
         return copies
 
     def others():
         return [a * 2 + 1 - core] + [((a + i) % SIDE) * 2 + g for i in range(1, SIDE) for g in range(2)]
 
-    def entries_arrived(t, q):
+    def entries_arrived(n, t, at, q=None):
+        cols, m = (pl.ds(0, 2), 0) if q is None else (pl.ds(q, 1), q)
         for k in others():
-            ref = e_all.at[t, q, k]
-            remote(ref, ref, as_sem.at[t, q, 0], ar_sem.at[t, q, k], sib).wait_recv()
+            ref = e_all.at[t, cols, k, at]
+            remote(ref, ref, as_sem.at[n, m, 0], ar_sem.at[n, m, k], sib).wait_recv()
 
     def b_copy(i, q):
         return remote(s2.at[q, i - 1], r2.at[q, i - 1], bs_sem.at[q, i - 1], br_sem.at[q, i - 1], along_b(i))
@@ -252,19 +256,27 @@
         for kind in range(2):
             z_direct(t, kind).start()
 
-    def multiply(t):
+    def multiply(t, blocks=(0, 3), sets=None):
+        low, high = blocks
+        at = slice(low * PART, high * PART)
+        left = x_all.at[t, low:high]
         for q in range(2):
             for own_half in range(2):
                 h = core if own_half else 1 - core
                 part = jnp.dot(
-                    x_all[t].reshape(ENTRIES, PIX), w4[h * 2 + q], preferred_element_type=F32
+                    left[...].reshape((high - low) * PART, PIX), w4[h * 2 + q], preferred_element_type=F32
                 ).astype(BF16)
                 if own_half:
-                    e_all[t, q, mine] = part
+                    e_all[t, q, mine, at] = part
                 else:
-                    o_all[t, q] = part
-            for c in entry_copies(t, q):
-                c.start()
+                    o_all[t, q, at] = part
+            if sets:
+                for c in entry_copies(sets[q][0], t, sets[q][1], q):
+                    c.start()
+
+    def send_entries(copies):
+        for c in copies:
+            c.start()
 
     def make_hits(t):
         row = tgt[pl.ds(t, 1), :]
@@ -279,60 +291,64 @@
             hits[blk], e_all[t, q].reshape(2 * SIDE * ENTRIES, QUART), preferred_element_type=F32
         )
 
+    def add_unit(t, q):
+        sums = jnp.dot(
+            hits[...].reshape(SIDE * 256, 2 * SIDE * ENTRIES),
+            e_all[t, q].reshape(2 * SIDE * ENTRIES, QUART),
+            preferred_element_type=F32,
+        )
+        acc2[q] += sums.reshape(SIDE, 256, QUART)
+
     def add_all(t):
         make_hits(t)
         for q in range(2):
-            entries_arrived(t, q)
-            sums = jnp.dot(
-                hits[...].reshape(SIDE * 256, 2 * SIDE * ENTRIES),
-                e_all[t, q].reshape(2 * SIDE * ENTRIES, QUART),
-                preferred_element_type=F32,
-            )
-            acc2[q] += sums.reshape(SIDE, 256, QUART)
-
-    acc2[...] = jnp.zeros_like(acc2)
+            entries_arrived(t, t, ALL, q)
+            add_unit(t, q)
+
     loads[0].wait()
     loads[1].wait()
+    normalize(0)
+    pl.semaphore_wait(barrier, len(partners))
+    z_start(0)
+    loads[2].wait()
+    loads[3].wait()
     for c in load_w:
         c.start()
-
-    @pl.loop(0, 2)
-    def _(t):
-        normalize(t)
-
-    pl.semaphore_wait(barrier, len(partners))
-    z_start(0)
+    normalize(1)
     z_start(1)
-    loads[2].wait()
-    loads[3].wait()
+    acc2[...] = jnp.zeros_like(acc2)
     send_halo()
     find_positions()
     for c in pos_copies:
         c.start()
 
-    @pl.loop(0, STEPS)
+    @pl.loop(2, STEPS)
     def _(t):
-        @pl.when(t == 2)
+        @pl.when(t == 4)
         def _():
             halo_up.wait_recv()
             halo_down.wait_recv()
             fill_halo()
 
-        @pl.when(t < STEPS - 2)
-        def _():
-            normalize(t + 2)
-            z_start(t + 2)
-
+        normalize(t)
+        z_start(t)
+
+    @pl.loop(0, STEPS)
+    def _(t):
         for kind in range(2):
             z_direct(t, kind).wait_recv()
-            z_forward(t, kind).start()
+
+        @pl.when(t < STEPS - 1)
+        def _():
+            for kind in range(2):
+                z_forward(t, kind).start()
 
         @pl.when(t == 0)
         def _():
             for c in load_w:
                 c.wait()
 
-        multiply(t)
+        multiply(t, sets=[(t, ALL)] * 2)
 
         @pl.when(t == 1)
         def _():
@@ -346,21 +362,28 @@
 
     end = UNITS - 1
 
-    def far(u):
-        for i in range(3):
+    def far(u, low, high):
+        for i in range(low, high):
             for kind in range(2):
                 z_forward((u - STEPS) * 3 + i, kind).wait_recv()
 
-    far(end - 1)
-    multiply(end - 1)
+    far(end - 1, 0, 3)
+    multiply(end - 1, sets=[(end - 1, ALL)] * 2)
+    for kind in range(2):
+        z_forward(STEPS - 3, kind).wait_send()
+        z_forward(STEPS - 1, kind).start()
     add_all(end - 2)
-    far(end)
-    multiply(end)
+    far(end, 0, 2)
+    multiply(end, (0, 2))
+    send_entries(entry_copies(end, end, EARLY))
+    far(end, 2, 3)
+    multiply(end, (2, 3), [(end + 1, LATE)] * 2)
     add_all(end - 1)
     make_hits(end)
+    entries_arrived(end, end, EARLY)
 
     for q in range(2):
-        entries_arrived(end, q)
+        entries_arrived(end + 1, end, LATE, q)
         for i in (2, 1, 3, 0):
             blk = (b + i) % SIDE
             add_entries(end, q, blk)
@@ -408,13 +431,23 @@
     def _(t):
         for kind in range(2):
             z_direct(t, kind).wait_send()
-            z_forward(t, kind).wait_send()
-
-    @pl.loop(0, UNITS)
+
+        @pl.when(t != STEPS - 3)
+        def _():
+            for kind in range(2):
+                z_forward(t, kind).wait_send()
+
+    @pl.loop(0, end)
     def _(t):
         for q in range(2):
-            for c in entry_copies(t, q):
+            for c in entry_copies(t, t, ALL, q):
                 c.wait_send()
+
+    for c in entry_copies(end, end, EARLY):
+        c.wait_send()
+    for q in range(2):
+        for c in entry_copies(end + 1, end, LATE, q):
+            c.wait_send()
 
     for q in range(2):
         for i in range(1, SIDE):
@@ -463,8 +496,8 @@
             dma((8,)),
             dma((STEPS, 4)),
             dma((STEPS, 4)),
-            dma((UNITS, 2, 7)),
-            dma((UNITS, 2, 8)),
+            dma((UNITS + 1, 2, 7)),
+            dma((UNITS + 1, 2, 8)),
             dma((2, 3)),
             dma((2, 3)),
             dma((2, 3)),

time: 96.4 us -> 92.9 us (0.964)
  Pallas kernels: 94.3 us -> 90.8 us
    pallas_call x1, Pallas kernels: 94.3 us -> 90.8 us  [shards(): pl.pallas_call(kernel, out_shape=jax.ShapeDtypeStruct((1, OWN, VOX), F32)...]
where the time goes in v3:
time: 92.9 us; the launch traced here: 92.7 us
  Pallas kernels  90.8 us (98%)
  local copies, waits for them, and re-layouts  1.89 us (2%)
    pallas_call x1, Pallas kernels, shards(): pl.pallas_call(kernel, out_shape=jax.ShapeDtypeStruct((1, OWN, VOX), F32)...  90.8 us
    unnamed x1, local copies, waits for them, and re-layouts  1.89 us

profile of v3, /device:TPU:1, one launch (start us, length us, event | category | flops | bytes accessed | tf_op | source)
XLA Modules:
  0.0 92.7 jit_solution(6782877074485051229)
XLA Ops:
  0.0 90.8 %shard_map.64 = f32[1,128,1024]{2,1,0:T(8,128)} custom-call(f32[8,96,1024]{2,1,0:T(8,128)} %px_hbm.1, s32[8,96,1024]{2,1,0:T(8,128)} %mk_hbm.1, bf16[1,4096,1024]{2,1,0:T(8,128)(2,1)} %w_hbm.1, s32[8,1,96]{2,1,0:T(1,128)} %bl_ref.1, s32[1,4096]{1,0:T(1,128)} %om_ref.1, s32[1,128]{1,0:T(1,128)} %mp_ref.1), custom_call_target="tpu_custom_call" | custom-call | tf_op jit(solution)/shard_map/pallas_call | solution.py:463
  90.8 1.9 %copy.8 = f32[1,128,1024]{2,1,0:T(8,128)} copy(f32[1,128,1024]{2,1,0:T(8,128)} %shard_map.64) | data formatting | bytes 1048576

commit v4 on v3

--- a/solution.py
+++ b/solution.py
@@ -54,7 +54,7 @@
 
 def kernel(
     px_hbm, mk_hbm, w_hbm, bl_ref, om_ref, mp_ref, out_ref,
-    px, mk, w4, corr, x_all, acc, o_all, e_all, acc2, hits, table, pos, pall, tgt,
+    px, mk, w4, corr, x_all, acc, o_all, e_all, acc2, hits, table, pos, pall, tgt, early_tgt, late_tgt, late_hits,
     hs, hr, s2, r2, fsum, tot, mir_in, own,
     ld_sem, lw_sem, hs_sem, hr_sem, ps_sem, pr_sem, zs_sem, zr_sem,
     as_sem, ar_sem, bs_sem, br_sem, fs_sem, fr_sem,
@@ -124,6 +124,8 @@
     halo_up = remote(hs.at[0], hr.at[0], hs_sem.at[0], hr_sem.at[0], up)
     halo_down = remote(hs.at[1], hr.at[1], hs_sem.at[1], hr_sem.at[1], down)
 
+    end = UNITS - 1
+
     def z_direct(t, kind):
         return remote(x_all.at[t, 0], x_all.at[t, 1 + kind], zs_sem.at[t, kind], zr_sem.at[t, kind], (up, down)[kind])
 
@@ -214,7 +216,11 @@
             to_a = jnp.where(core == 0, owner >> 3, (owner >> 1) & 3)
             to_b = jnp.where(core == 0, (owner >> 1) & 3, owner >> 3)
             row = ((to_b * 2 + (owner & 1)) << 7) + (at & 127)
-            tgt[:, k * ENTRIES : (k + 1) * ENTRIES] = jnp.where(to_a == a, row, -1)[:, :ENTRIES]
+            row = jnp.where(to_a == a, row, -1)
+            tgt[:, k * ENTRIES : (k + 1) * ENTRIES] = row[:, :ENTRIES]
+            cut = 2 * PART
+            early_tgt[:, k * cut : (k + 1) * cut] = row[:, :cut]
+            late_tgt[:, k * PART : (k + 1) * PART] = row[:, cut:ENTRIES]
 
     def send_halo():
         for f in range(FRAMES):
@@ -286,10 +292,30 @@
             hit = (lax.broadcasted_iota(I32, (256, 2 * SIDE * ENTRIES), 0) + blk * 256) == row
             hits[blk] = hit.astype(F32).astype(BF16)
 
-    def add_entries(t, q, blk):
-        acc2[q, blk] += jnp.dot(
-            hits[blk], e_all[t, q].reshape(2 * SIDE * ENTRIES, QUART), preferred_element_type=F32
-        )
+    def add_early():
+        n = 4 * SIDE * PART
+        row = early_tgt[pl.ds(end, 1), :]
+
+        @pl.loop(0, SIDE)
+        def _(blk):
+            hit = (lax.broadcasted_iota(I32, (256, n), 0) + blk * 256) == row
+            hits[blk, :, 0:n] = hit.astype(F32).astype(BF16)
+
+        entries_arrived(end, end, EARLY)
+        for q in range(2):
+            terms = e_all[end, q, :, 0 : 2 * PART].reshape(n, QUART)
+            sums = jnp.dot(hits[:, :, 0:n].reshape(SIDE * 256, n), terms, preferred_element_type=F32)
+            acc2[q] += sums.reshape(SIDE, 256, QUART)
+
+    def make_late_hits():
+        row = late_tgt[pl.ds(end, 1), :]
+        hit = lax.broadcasted_iota(I32, (SIDE * 256, 2 * SIDE * PART), 0) == row
+        late_hits[...] = hit.astype(F32).astype(BF16)
+
+    def add_late(q):
+        terms = e_all[end, q, :, 2 * PART : ENTRIES].reshape(2 * SIDE * PART, QUART)
+        sums = jnp.dot(late_hits[...], terms, preferred_element_type=F32)
+        acc2[q] += sums.reshape(SIDE, 256, QUART)
 
     def add_unit(t, q):
         sums = jnp.dot(
@@ -360,7 +386,6 @@
         def _():
             add_all(t - 1)
 
-    end = UNITS - 1
 
     def far(u, low, high):
         for i in range(low, high):
@@ -379,48 +404,47 @@
     far(end, 2, 3)
     multiply(end, (2, 3), [(end + 1, LATE)] * 2)
     add_all(end - 1)
-    make_hits(end)
-    entries_arrived(end, end, EARLY)
+    add_early()
+    make_late_hits()
 
     for q in range(2):
         entries_arrived(end + 1, end, LATE, q)
-        for i in (2, 1, 3, 0):
-            blk = (b + i) % SIDE
-            add_entries(end, q, blk)
-            if i:
-                s2[q, i - 1] = acc2[q, blk].astype(BF16)
-                b_copy(i, q).start()
-    for q in range(2):
+        add_late(q)
+        for p in (2 * q, 2 * q + 1):
+            at = slice((p % 2) * OWN, (p % 2 + 1) * OWN)
+            for i in (2, 1, 3):
+                s2[p, i - 1] = acc2[q, (b + i) % SIDE, :, at].astype(BF16)
+                b_copy(i, p).start()
+    for p in range(4):
         for i in range(1, SIDE):
-            b_copy(i, q).wait_recv()
-        total = acc2[q, b] + (r2[q, 0].astype(F32) + r2[q, 1].astype(F32) + r2[q, 2].astype(F32))
-        tot[q] = total
+            b_copy(i, p).wait_recv()
+        at = slice((p % 2) * OWN, (p % 2 + 1) * OWN)
+        total = acc2[p // 2, b, :, at] + (r2[p, 0].astype(F32) + r2[p, 1].astype(F32) + r2[p, 2].astype(F32))
+        tot[p] = total
         for cc in range(2):
-            fsum[q, cc] = total[cc * OWN : (cc + 1) * OWN, :].astype(BF16)
-        for c in last_copies(q):
+            fsum[p, cc] = total[cc * OWN : (cc + 1) * OWN, :].astype(BF16)
+        for c in last_copies(p):
             c.start()
-        own[core, q] = tot[q, pl.ds(pl.multiple_of(core * OWN, OWN), OWN), :]
+        own[core, p] = tot[p, pl.ds(pl.multiple_of(core * OWN, OWN), OWN), :]
     pick = (lax.broadcasted_iota(I32, (OWN, OWN), 0) == mp_ref[...]).astype(F32).astype(BF16)
     flip = (
         lax.broadcasted_iota(I32, (OWN, OWN), 0) + lax.broadcasted_iota(I32, (OWN, OWN), 1) == OWN - 1
     ).astype(F32).astype(BF16)
-    for q in range(2):
-        remote(own.at[0, q], own.at[0, q], fs_sem.at[q, 2], fr_sem.at[q, 2], sib).wait_recv()
+    for p in range(4):
+        remote(own.at[0, p], own.at[0, p], fs_sem.at[p, 2], fr_sem.at[p, 2], sib).wait_recv()
         for h in range(2):
-            ref = mir_in.at[h, q]
-            remote(ref, ref, fs_sem.at[q, 0], fr_sem.at[q, h], dev(x, y, 0, z_far)).wait_recv()
+            ref = mir_in.at[h, p]
+            remote(ref, ref, fs_sem.at[p, 0], fr_sem.at[p, h], dev(x, y, 0, z_far)).wait_recv()
         for h in range(2):
             rows = lax.dot_general(
-                pick, mir_in[1 - h, q], (((0,), (0,)), ((), ())), preferred_element_type=F32
+                pick, mir_in[1 - h, p], (((0,), (0,)), ((), ())), preferred_element_type=F32
             ).astype(BF16)
-            for v in range(2):
-                turned = jnp.dot(rows[:, (1 - v) * OWN : (2 - v) * OWN], flip, preferred_element_type=F32)
-                at = h * HALF + (1 - q) * QUART + v * OWN
-                out_ref[0, :, at : at + OWN] = turned
-    for q in range(2):
+            at = h * HALF + (3 - p) * OWN
+            out_ref[0, :, at : at + OWN] = jnp.dot(rows, flip, preferred_element_type=F32)
+    for p in range(4):
         for h in range(2):
-            at = slice(h * HALF + q * QUART, h * HALF + (q + 1) * QUART)
-            out_ref[0, :, at] = 0.5 * (own[h, q] + out_ref[0, :, at])
+            at = slice(h * HALF + p * OWN, h * HALF + (p + 1) * OWN)
+            out_ref[0, :, at] = 0.5 * (own[h, p] + out_ref[0, :, at])
 
     halo_up.wait_send()
     halo_down.wait_send()
@@ -449,10 +473,10 @@
         for c in entry_copies(end + 1, end, LATE, q):
             c.wait_send()
 
-    for q in range(2):
+    for p in range(4):
         for i in range(1, SIDE):
-            b_copy(i, q).wait_send()
-        for c in last_copies(q):
+            b_copy(i, p).wait_send()
+        for c in last_copies(p):
             c.wait_send()
 
 
@@ -480,14 +504,17 @@
             pltpu.VMEM((8, 128), I32),
             pltpu.VMEM((2 * SIDE, 8, 128), I32),
             pltpu.VMEM((8, 2 * SIDE * ENTRIES), I32),
+            pltpu.VMEM((8, 4 * SIDE * PART), I32),
+            pltpu.VMEM((8, 2 * SIDE * PART), I32),
+            pltpu.VMEM((SIDE * 256, 2 * SIDE * PART), BF16),
             pltpu.VMEM((2, FRAMES // 2, 8, COLS), F32),
             pltpu.VMEM((2, FRAMES // 2, 8, COLS), F32),
-            pltpu.VMEM((2, 3, 256, QUART), BF16),
-            pltpu.VMEM((2, 3, 256, QUART), BF16),
-            pltpu.VMEM((2, 2, OWN, QUART), BF16),
-            pltpu.VMEM((2, 256, QUART), F32),
-            pltpu.VMEM((2, 2, OWN, QUART), BF16),
-            pltpu.VMEM((2, 2, OWN, QUART), F32),
+            pltpu.VMEM((4, 3, 256, OWN), BF16),
+            pltpu.VMEM((4, 3, 256, OWN), BF16),
+            pltpu.VMEM((4, 2, OWN, OWN), BF16),
+            pltpu.VMEM((4, 256, OWN), F32),
+            pltpu.VMEM((2, 4, OWN, OWN), BF16),
+            pltpu.VMEM((2, 4, OWN, OWN), F32),
             dma((4,)),
             dma((4,)),
             dma((2,)),
@@ -498,10 +525,10 @@
             dma((STEPS, 4)),
             dma((UNITS + 1, 2, 7)),
             dma((UNITS + 1, 2, 8)),
-            dma((2, 3)),
-            dma((2, 3)),
-            dma((2, 3)),
-            dma((2, 3)),
+            dma((4, 3)),
+            dma((4, 3)),
+            dma((4, 3)),
+            dma((4, 3)),
         ],
         compiler_params=pltpu.CompilerParams(
             collective_id=0, has_side_effects=True, vmem_limit_bytes=60 * 1024 * 1024

time: 92.9 us -> 92.6 us (level)
  no operation moved by 1% of the time
where the time goes in v4:
time: 92.6 us; the launch traced here: 92.4 us
  Pallas kernels  90.5 us (98%)
  local copies, waits for them, and re-layouts  1.89 us (2%)
    pallas_call x1, Pallas kernels, shards(): pl.pallas_call(kernel, out_shape=jax.ShapeDtypeStruct((1, OWN, VOX), F32)...  90.5 us
    unnamed x1, local copies, waits for them, and re-layouts  1.89 us

profile of v4, /device:TPU:1, one launch (start us, length us, event | category | flops | bytes accessed | tf_op | source)
XLA Modules:
  0.0 92.4 jit_solution(6336289559099127381)
XLA Ops:
  0.0 90.5 %shard_map.64 = f32[1,128,1024]{2,1,0:T(8,128)} custom-call(f32[8,96,1024]{2,1,0:T(8,128)} %px_hbm.1, s32[8,96,1024]{2,1,0:T(8,128)} %mk_hbm.1, bf16[1,4096,1024]{2,1,0:T(8,128)(2,1)} %w_hbm.1, s32[8,1,96]{2,1,0:T(1,128)} %bl_ref.1, s32[1,4096]{1,0:T(1,128)} %om_ref.1, s32[1,128]{1,0:T(1,128)} %mp_ref.1), custom_call_target="tpu_custom_call" | custom-call | tf_op jit(solution)/shard_map/pallas_call | solution.py:487
  90.5 1.9 %copy.8 = f32[1,128,1024]{2,1,0:T(8,128)} copy(f32[1,128,1024]{2,1,0:T(8,128)} %shard_map.64) | data formatting | bytes 1048576

commit v5 on v4

--- a/solution.py
+++ b/solution.py
@@ -276,9 +276,10 @@
                     e_all[t, q, mine, at] = part
                 else:
                     o_all[t, q, at] = part
-            if sets:
-                for c in entry_copies(sets[q][0], t, sets[q][1], q):
-                    c.start()
+                if sets:
+                    copies = entry_copies(sets[q][0], t, sets[q][1], q)
+                    for i in (5, 4, 6) if own_half else (2, 1, 3, 0):
+                        copies[i].start()
 
     def send_entries(copies):
         for c in copies:

time: 92.6 us -> 96.2 us (1.039)
  Pallas kernels: 90.5 us -> 94.1 us
    pallas_call x1, Pallas kernels: 90.5 us -> 94.1 us  [shards(): pl.pallas_call(kernel, out_shape=jax.ShapeDtypeStruct((1, OWN, VOX), F32)...]
where the time goes in v5:
time: 96.2 us; the launch traced here: 96 us
  Pallas kernels  94.1 us (98%)
  local copies, waits for them, and re-layouts  1.89 us (2%)
    pallas_call x1, Pallas kernels, shards(): pl.pallas_call(kernel, out_shape=jax.ShapeDtypeStruct((1, OWN, VOX), F32)...  94.1 us

profile of v5, /device:TPU:1, one launch (start us, length us, event | category | flops | bytes accessed | tf_op | source)
XLA Modules:
  0.0 96.0 jit_solution(14111031009428887857)
XLA Ops:
  0.0 94.1 %shard_map.64 = f32[1,128,1024]{2,1,0:T(8,128)} custom-call(f32[8,96,1024]{2,1,0:T(8,128)} %px_hbm.1, s32[8,96,1024]{2,1,0:T(8,128)} %mk_hbm.1, bf16[1,4096,1024]{2,1,0:T(8,128)(2,1)} %w_hbm.1, s32[8,1,96]{2,1,0:T(1,128)} %bl_ref.1, s32[1,4096]{1,0:T(1,128)} %om_ref.1, s32[1,128]{1,0:T(1,128)} %mp_ref.1), custom_call_target="tpu_custom_call" | custom-call | tf_op jit(solution)/shard_map/pallas_call | solution.py:488
  94.1 1.9 %copy.8 = f32[1,128,1024]{2,1,0:T(8,128)} copy(f32[1,128,1024]{2,1,0:T(8,128)} %shard_map.64) | data formatting | bytes 1048576

commit v6 on v4

--- a/solution.py
+++ b/solution.py
@@ -276,7 +276,8 @@
                     e_all[t, q, mine, at] = part
                 else:
                     o_all[t, q, at] = part
-            if sets:
+        if sets:
+            for q in range(2):
                 for c in entry_copies(sets[q][0], t, sets[q][1], q):
                     c.start()
 

time: 92.6 us -> 94.5 us (1.021)
  Pallas kernels: 90.5 us -> 92.4 us
    pallas_call x1, Pallas kernels: 90.5 us -> 92.4 us  [shards(): pl.pallas_call(kernel, out_shape=jax.ShapeDtypeStruct((1, OWN, VOX), F32)...]
where the time goes in v6:
time: 94.5 us; the launch traced here: 94.3 us
  Pallas kernels  92.4 us (98%)
  local copies, waits for them, and re-layouts  1.89 us (2%)
    pallas_call x1, Pallas kernels, shards(): pl.pallas_call(kernel, out_shape=jax.ShapeDtypeStruct((1, OWN, VOX), F32)...  92.4 us

profile of v6, /device:TPU:1, one launch (start us, length us, event | category | flops | bytes accessed | tf_op | source)
XLA Modules:
  0.0 94.3 jit_solution(4266037407831809863)
XLA Ops:
  0.0 92.4 %shard_map.64 = f32[1,128,1024]{2,1,0:T(8,128)} custom-call(f32[8,96,1024]{2,1,0:T(8,128)} %px_hbm.1, s32[8,96,1024]{2,1,0:T(8,128)} %mk_hbm.1, bf16[1,4096,1024]{2,1,0:T(8,128)(2,1)} %w_hbm.1, s32[8,1,96]{2,1,0:T(1,128)} %bl_ref.1, s32[1,4096]{1,0:T(1,128)} %om_ref.1, s32[1,128]{1,0:T(1,128)} %mp_ref.1), custom_call_target="tpu_custom_call" | custom-call | tf_op jit(solution)/shard_map/pallas_call | solution.py:488
  92.4 1.9 %copy.8 = f32[1,128,1024]{2,1,0:T(8,128)} copy(f32[1,128,1024]{2,1,0:T(8,128)} %shard_map.64) | data formatting | bytes 1048576
